TPU v7x, 32 devices: a whole 2x2x4 slice. The times are simulated.
32 devices in a mesh: long: 16 (over z, y, x), short: 2 (over core).
Axes of the slice: x: 2, y: 2, z: 4, core: 2. Of those that a mesh axis runs over, the one named last changes fastest.
Arguments:
- outer_block: bfloat16 [2, 16, 2, 512, 512], P('short', 'long'), may hold values from -0.15625 to 0.15625
- outflow_block: bfloat16 [2, 16, 2, 512, 512], P('short', 'long'), may hold values from -0.15625 to 0.15625
- inflow_block: bfloat16 [2, 16, 2, 512, 512], P('short', 'long'), may hold values from -0.15625 to 0.15625
- shared_block: bfloat16 [2, 16, 2, 512, 512], P('short', 'long'), may hold values from -1 to 1
Outputs:
- own_block: float32 [2, 2, 512, 4096], P('short', None, None, 'long')
- cross_block: float32 [2, 2, 512, 4096], P('short', None, None, 'long')
All inputs are finite; a program needn't handle non-finite values.
Results may differ from a plain program's by a relative error of at most 0.0095.
Values may be sent and summed in bfloat16 or wider, within the bound.
No kernel may reach another device: no remote copies, remote signals or barrier semaphores. Data moves between devices by JAX's collectives and lax.ppermute only.
A program may use at most 64 MiB of HBM per device.

v0:
```python
import functools
import math

import jax
import jax.numpy as jnp
from jax import lax
from jax.experimental import pallas as pl
from jax.experimental.pallas import tpu as pltpu
from jax.sharding import PartitionSpec as P


BF = jnp.bfloat16
F32 = jnp.float32


def across(x, axis, parity):
    return lax.ppermute(x, axis, [(i, i ^ 1) for i in range(lax.axis_size(axis)) if i % 2 == parity])


def swap(x, axis):
    return lax.ppermute(x, axis, [(i, i ^ 1) for i in range(lax.axis_size(axis))])


def cstage(left, right, emit):
    k, m = right.shape[1], right.shape[2]
    re, im = left[0], left[1]
    column = right[...].reshape(2 * k, m)
    upper = jnp.dot(jnp.concatenate([re, -im], axis=1), column, preferred_element_type=F32)
    lower = jnp.dot(jnp.concatenate([im, re], axis=1), column, preferred_element_type=F32)
    emit(upper, lower)


def cstage_two(left, right, left_b, right_b, emit):
    k, m = right.shape[1], right.shape[2]
    column, column_b = right[...].reshape(2 * k, m), right_b[...].reshape(2 * k, m)
    upper = jnp.dot(jnp.concatenate([left[0], -left[1]], axis=1), column, preferred_element_type=F32)
    upper += jnp.dot(jnp.concatenate([left_b[0], -left_b[1]], axis=1), column_b, preferred_element_type=F32)
    lower = jnp.dot(jnp.concatenate([left[1], left[0]], axis=1), column, preferred_element_type=F32)
    lower += jnp.dot(jnp.concatenate([left_b[1], left_b[0]], axis=1), column_b, preferred_element_type=F32)
    emit(upper, lower)


def plain(dst):
    def emit(re, im):
        dst[0] = re.astype(dst.dtype)
        dst[1] = im.astype(dst.dtype)

    return emit


def plus(dst, base):
    def emit(re, im):
        dst[0] = (base[0].astype(F32) + re).astype(dst.dtype)
        dst[1] = (base[1].astype(F32) + im).astype(dst.dtype)

    return emit


def level_one(t, h, hr, g, f, e, p, s, d, v, m):
    cstage(h, hr, plain(p))
    cstage(p, g, plus(v, g))
    cstage(p, v, plus(s, g))
    cstage(hr, s, plain(m))
    cstage(f, m, plus(d, e))


def gate(x, t):
    t[...] = x[...]


def second_product(d, df, q):
    cstage(d, df, plain(q))


def columns(h, hr, p, f, g, q, df, s, sf, xy, k32, kb, v1, sb, c, w1, w, z):
    def emit_k(re, im):
        k32[0], k32[1] = re, im
        kb[0], kb[1] = re.astype(BF), im.astype(BF)

    cstage(h, g, emit_k)
    cstage(p, kb, plus(v1, k32))
    cstage(hr, v1, plus(sb, g))
    cstage(f, sb, plain(c))
    cstage(q, c, plus(w1, c))
    cstage(q, w1, plus(w, c))
    cstage(df, w, plain(z))
    cstage_two(p, v1, s, z, plus(xy.at[0], k32))
    cstage(sf, w, plain(xy.at[1]))


def last(factor, flag, f_l, ff_l, xy_l, f_r, ff_r, xy_r, e_r, own, far, f, ff, xy, e, sems):
    def fetch(sources):
        copies = [pltpu.make_async_copy(a, b, sems.at[i]) for i, (a, b) in enumerate(sources)]
        for c in copies:
            c.start()
        for c in copies:
            c.wait()

    half = e.shape[2]

    @pl.when(flag[0] == 1)
    def _():
        fetch([(f_l, f), (ff_l, ff), (xy_l, xy)])
        e[...] = jnp.zeros_like(e)

    @pl.when(flag[0] == 0)
    def _():
        fetch([(f_r, f), (ff_r, ff), (xy_r, xy), (e_r.at[:, :, pl.ds(half, half)], e)])

    def scaled(dst, base=None):
        def emit(re, im):
            if base is not None:
                re, im = base[0].astype(F32) + re, base[1].astype(F32) + im
            dst[0], dst[1] = re * factor, im * factor

        return emit

    cstage(f, xy.at[0], scaled(own, e))
    cstage(ff, xy.at[1], scaled(far))


def finish(factor, first, own, e, *rest):
    out, buf, sems = rest[-3:]
    copies = []
    for c in range(2):
        r = pl.ds(first, e.shape[1])
        buf[c] = own[c, r, :] + e[c].astype(F32) * factor
        copies.append(pltpu.make_async_copy(buf.at[c], out.at[c, r, :], sems.at[c]))
        copies[-1].start()
    for c in copies:
        c.wait()


def call(body, outs, args, units, scratch=(), specs=None, out_spec=None, aliases=None):
    n = args[-1].shape[1] if units else 0
    vmem = pl.BlockSpec(memory_space=pltpu.VMEM)
    return pl.pallas_call(
        body,
        out_shape=[jax.ShapeDtypeStruct(s, t) for s, t in outs],
        in_specs=specs or [vmem] * len(args),
        out_specs=[out_spec or vmem] * len(outs),
        scratch_shapes=[pltpu.VMEM(*s) if isinstance(s, tuple) else s for s in scratch],
        cost_estimate=pl.CostEstimate(
            flops=int(8 * n * n * n * units),
            bytes_accessed=4 * n * n * (len(args) + len(outs)),
            transcendentals=0,
        ),
        compiler_params=pltpu.CompilerParams(vmem_limit_bytes=24 << 20),
        input_output_aliases=aliases or {},
    )(*args)


def shards(outer_block, outflow_block, inflow_block, shared_block):
    outer, outflow, inflow, shared = outer_block[0, 0], outflow_block[0, 0], inflow_block[0, 0], shared_block[0, 0]
    n = outer.shape[2]
    half = n // 2
    factor = math.sqrt(n)
    full, part = (2, n, n), (2, n, half)

    shared_r = across(shared, "long", 1)
    inflow_r1 = across(inflow[:, :, half:], "long", 1)
    inflow_r0 = across(inflow[:, :, :half], "long", 1)
    outflow_r = across(outflow, "long", 1)
    cut = n * 3 // 4
    outer_r0 = across(outer[:, :cut, :half], "long", 1)
    outer_r1 = across(outer[:, cut:, :half], "long", 1)
    outflow_far = swap(outflow, "short")

    token = pl.pallas_call(
        gate,
        grid=(1,),
        out_shape=jax.ShapeDtypeStruct((1, 16, 128), BF),
        in_specs=[pl.BlockSpec((1, 16, 128), lambda i: (0, 0, 0))],
        out_specs=pl.BlockSpec((1, 16, 128), lambda i: (0, 0, 0)),
        name="gate",
    )(outer)
    product, series, diag = call(
        level_one, [(full, BF)] * 3, (token, shared, shared_r, inflow, outflow, outer), 5, [(full, BF)] * 2
    )
    diag_far = swap(diag, "short")
    series_far = swap(series, "short")
    (product_two,) = call(second_product, [(full, BF)], (diag, diag_far), 1)

    def half_columns(g):
        return call(
            columns,
            [((2,) + part, BF)],
            (shared, shared_r, product, outflow, g, product_two, diag_far, series, series_far),
            5,
            [(part, F32)] + [(part, BF)] * 7,
        )[0]

    xy1 = half_columns(inflow_r1)
    xy1_r = across(xy1, "long", 0)
    xy0 = half_columns(inflow_r0)

    outflow_r_far = swap(outflow_r, "short")
    flag = (lax.axis_index("long") % 2 == 0).astype(jnp.int32).reshape(1)
    hbm = pl.BlockSpec(memory_space=pltpu.HBM)
    own, far = call(
        functools.partial(last, factor),
        [(part, F32)] * 2,
        (flag, outflow_r, outflow_r_far, xy0, outflow, outflow_far, xy1_r, outer),
        1,
        [(full, BF), (full, BF), ((2,) + part, BF), (part, BF), pltpu.SemaphoreType.DMA((4,))],
        [pl.BlockSpec(memory_space=pltpu.SMEM)] + [hbm] * 7,
    )

    def add(first, rows, *more):
        return call(
            functools.partial(finish, factor, first),
            [(part, F32)],
            (own,) + rows + more,
            0,
            [((2,) + rows[0].shape[1:], F32), pltpu.SemaphoreType.DMA((2,))],
            [pl.BlockSpec(memory_space=pltpu.VMEM)] * 2 + [hbm] * len(more),
            hbm,
            {2: 0} if more else None,
        )[0]

    partly = add(0, (outer_r0,))
    own = add(cut, (outer_r1,), partly)
    return own[None], far[None]


def solution(mesh):
    spec = P("short", "long", None, None, None)
    out = P("short", None, None, "long")
    return jax.shard_map(shards, mesh=mesh, in_specs=(spec,) * 4, out_specs=(out, out), check_vma=False)
```

profile of v0, /device:TPU:6, one launch (start us, length us, event | category | flops | bytes accessed | tf_op | source)
XLA Modules:
  0.0 114.0 jit_solution(1528699703573399457)
XLA Ops:
  0.6 2.6 %collective-permute-start.2 = (bf16[2,512,512]{2,1,0:T(8,128)(2,1)}, bf16[2,512,512]{2,1,0:T(8,128)(2,1)S(1)}, u32[]{:S(2)}, u32[]{:S(2)}) collective-permute-start(bf16[2,512,512]{2,1,0:T(8,128)(2,1)} %bitcast.14), channel_id=1, source_target_pairs={{2,0},{6,4},{10,8},{14,12},{18,16},{22,20},{26,24},{30,28},{3,1},{... | collective-permute-start | bytes 3145736 | tf_op jit(solution)/shard_map/ppermute | solution.py:17
  3.3 1.4 %collective-permute-start = (bf16[2,512,512]{2,1,0:T(8,128)(2,1)}, bf16[2,512,512]{2,1,0:T(8,128)(2,1)S(1)}, u32[]{:S(2)}, u32[]{:S(2)}) collective-permute-start(bf16[2,512,512]{2,1,0:T(8,128)(2,1)} %bitcast.1.f.f_r), channel_id=1, source_target_pairs={{2,0},{6,4},{10,8},{14,12},{18,16},{22,20},{26,24},{30,28},{3,1},{... | collective-permute-start | bytes 3145736 | tf_op jit(solution)/shard_map/ppermute | solution.py:17
  4.7 1.3 %gate.1.t = bf16[1,16,128]{2,1,0:T(8,128)(2,1)} custom-call(bf16[2,512,512]{2,1,0:T(8,128)(2,1)} %bitcast.7), custom_call_target="tpu_custom_call" | custom-call | tf_op jit(solution)/shard_map/gate/pallas_call | solution.py:169
  5.9 21.1 %collective-permute-done.2.hr = bf16[2,512,512]{2,1,0:T(8,128)(2,1)S(1)} collective-permute-done((bf16[2,512,512]{2,1,0:T(8,128)(2,1)}, bf16[2,512,512]{2,1,0:T(8,128)(2,1)S(1)}, u32[]{:S(2)}, u32[]{:S(2)}) %collective-permute-start.2) | collective-permute-done | bytes 1048608 | tf_op jit(solution)/shard_map/ppermute | solution.py:17
  27.1 1.6 %copy-done.1 = bf16[1,1,2,512,512]{4,3,2,1,0:T(8,128)(2,1)S(1)} copy-done((bf16[1,1,2,512,512]{4,3,2,1,0:T(8,128)(2,1)S(1)}, bf16[1,1,2,512,512]{4,3,2,1,0:T(8,128)(2,1)}, u32[]{:S(2)}) %copy-start.1) | copy-done | bytes 1048600
  28.7 0.7 copy-done.2
  29.4 1.2 %copy-done.3 = bf16[1,1,2,512,512]{4,3,2,1,0:T(8,128)(2,1)S(1)} copy-done((bf16[1,1,2,512,512]{4,3,2,1,0:T(8,128)(2,1)S(1)}, bf16[1,1,2,512,512]{4,3,2,1,0:T(8,128)(2,1)}, u32[]{:S(2)}) %copy-start.3) | copy-done | bytes 1048600
  30.6 6.9 %shard_map.59 = (bf16[2,512,512]{2,1,0:T(8,128)(2,1)S(1)}, bf16[2,512,512]{2,1,0:T(8,128)(2,1)S(1)}, bf16[2,512,512]{2,1,0:T(8,128)(2,1)S(1)}) custom-call(bf16[1,16,128]{2,1,0:T(8,128)(2,1)S(1)} %copy-done.2, bf16[2,512,512]{2,1,0:T(8,128)(2,1)S(1)} %bitcast.15, bf16[2,512,512]{2,1,0:T(8,128)(2,1)S(1)} %collective-permute-done.2.hr, ...), custom_call_target="tpu_custom_call" | custom-call | flops 5368709120 | bytes 9437184 | tf_op jit(solution)/shard_map/pallas_call | solution.py:137
  37.5 0.0 copy-start.17
  37.5 0.1 collective-permute-start.4
  37.6 0.5 collective-permute-start.5
  38.1 0.9 fusion
  39.0 4.4 %collective-permute-start.7 = (bf16[2,512,256]{2,1,0:T(8,128)(2,1)S(1)}, bf16[2,512,256]{2,1,0:T(8,128)(2,1)S(1)}, u32[]{:S(2)}, u32[]{:S(2)}) collective-permute-start(bf16[2,512,256]{2,1,0:T(8,128)(2,1)S(1)} %get-tuple-element.12), channel_id=1, source_target_pairs={{2,0},{6,4},{10,8},{14,12},{18,16},{22,20},{26,24},{30,28},{3,1},{... | collective-permute-start | bytes 1572872 | tf_op jit(solution)/shard_map/ppermute | solution.py:17
  43.4 0.1 collective-permute-start.6
  43.5 6.0 %collective-permute-done.f_l = bf16[2,512,512]{2,1,0:T(8,128)(2,1)S(1)} collective-permute-done((bf16[2,512,512]{2,1,0:T(8,128)(2,1)}, bf16[2,512,512]{2,1,0:T(8,128)(2,1)S(1)}, u32[]{:S(2)}, u32[]{:S(2)}) %collective-permute-start) | collective-permute-done | bytes 1048608 | tf_op jit(solution)/shard_map/ppermute | solution.py:17
  49.5 0.0 collective-permute-start.1
  49.5 0.0 collective-permute-done.4.df
  49.5 1.2 %shard_map.60.q = bf16[2,512,512]{2,1,0:T(8,128)(2,1)S(1)} custom-call(bf16[2,512,512]{2,1,0:T(8,128)(2,1)S(1)} %get-tuple-element.8.d, bf16[2,512,512]{2,1,0:T(8,128)(2,1)S(1)} %collective-permute-done.4.df), custom_call_target="tpu_custom_call" | custom-call | flops 1073741824 | bytes 3145728 | tf_op jit(solution)/shard_map/pallas_call | solution.py:137
  50.8 8.7 %collective-permute-done.7.g = bf16[2,512,256]{2,1,0:T(8,128)(2,1)S(1)} collective-permute-done((bf16[2,512,256]{2,1,0:T(8,128)(2,1)S(1)}, bf16[2,512,256]{2,1,0:T(8,128)(2,1)S(1)}, u32[]{:S(2)}, u32[]{:S(2)}) %collective-permute-start.7) | collective-permute-done | bytes 524320 | tf_op jit(solution)/shard_map/ppermute | solution.py:17
  59.5 0.0 collective-permute-done.5.sf
  59.5 0.0 copy-done.17
  59.5 0.0 copy-done.11
  59.6 0.0 copy-done.4
  59.6 8.7 %shard_map.62 = bf16[2,2,512,256]{3,2,1,0:T(8,128)(2,1)} custom-call(bf16[2,512,512]{2,1,0:T(8,128)(2,1)S(1)} %bitcast.16, bf16[2,512,512]{2,1,0:T(8,128)(2,1)S(1)} %copy-done.7, bf16[2,512,512]{2,1,0:T(8,128)(2,1)S(1)} %get-tuple-element.7.p, bf16[2,512,512]{2,1,0:T(8,128)(2,1)} %bitcast.1.f.f_r, bf16[2,512,256]{2,1,0:T(8,128)(2,1)S(1)} %collective-permute-done.7.g, ...), custom_call_target="tpu_custom_call" | custom-call | flops 5368709120 | bytes 10485760 | tf_op jit(solution)/shard_map/pallas_call | solution.py:137
  68.3 1.3 %collective-permute-start.8 = (bf16[2,2,512,256]{3,2,1,0:T(8,128)(2,1)}, bf16[2,2,512,256]{3,2,1,0:T(8,128)(2,1)}, u32[]{:S(2)}, u32[]{:S(2)}) collective-permute-start(bf16[2,2,512,256]{3,2,1,0:T(8,128)(2,1)} %shard_map.62), channel_id=1, source_target_pairs={{0,2},{4,6},{8,10},{12,14},{16,18},{20,22},{24,26},{28,30},{1,3},{... | collective-permute-start | bytes 3145736 | tf_op jit(solution)/shard_map/ppermute | solution.py:17
  69.6 6.4 %collective-permute-start.3 = (bf16[2,512,256]{2,1,0:T(8,128)(2,1)}, bf16[2,512,256]{2,1,0:T(8,128)(2,1)}, u32[]{:S(2)}, u32[]{:S(2)}) collective-permute-start(bf16[2,512,256]{2,1,0:T(8,128)(2,1)} %get-tuple-element.13), channel_id=1, source_target_pairs={{2,0},{6,4},{10,8},{14,12},{18,16},{22,20},{26,24},{30,28},{3,1},{... | collective-permute-start | bytes 1572872 | tf_op jit(solution)/shard_map/ppermute | solution.py:17
  75.9 0.8 slice.19
  76.8 1.3 %collective-permute-start.10 = (bf16[2,384,256]{2,1,0:T(8,128)(2,1)}, bf16[2,384,256]{2,1,0:T(8,128)(2,1)S(1)}, u32[]{:S(2)}, u32[]{:S(2)}) collective-permute-start(bf16[2,384,256]{2,1,0:T(8,128)(2,1)} %slice.19), channel_id=1, source_target_pairs={{2,0},{6,4},{10,8},{14,12},{18,16},{22,20},{26,24},{30,28},{3,1},{... | collective-permute-start | bytes 1179656 | tf_op jit(solution)/shard_map/ppermute | solution.py:17
  78.1 0.7 slice.18
  78.8 8.9 %collective-permute-done.3.g = bf16[2,512,256]{2,1,0:T(8,128)(2,1)} collective-permute-done((bf16[2,512,256]{2,1,0:T(8,128)(2,1)}, bf16[2,512,256]{2,1,0:T(8,128)(2,1)}, u32[]{:S(2)}, u32[]{:S(2)}) %collective-permute-start.3) | collective-permute-done | bytes 524320 | tf_op jit(solution)/shard_map/ppermute | solution.py:17
  87.7 4.6 %collective-permute-start.9 = (bf16[2,128,256]{2,1,0:T(8,128)(2,1)}, bf16[2,128,256]{2,1,0:T(8,128)(2,1)S(1)}, u32[]{:S(2)}, u32[]{:S(2)}) collective-permute-start(bf16[2,128,256]{2,1,0:T(8,128)(2,1)} %slice.18), channel_id=1, source_target_pairs={{2,0},{6,4},{10,8},{14,12},{18,16},{22,20},{26,24},{30,28},{3,1},{... | collective-permute-start | bytes 393224 | tf_op jit(solution)/shard_map/ppermute | solution.py:17
  92.3 0.0 copy-start.5
  92.3 1.2 %copy-done.5 = bf16[1,1,2,512,512]{4,3,2,1,0:T(8,128)(2,1)S(1)} copy-done((bf16[1,1,2,512,512]{4,3,2,1,0:T(8,128)(2,1)S(1)}, bf16[1,1,2,512,512]{4,3,2,1,0:T(8,128)(2,1)}, u32[]{:S(2)}) %copy-start.5) | copy-done | bytes 1048600
  93.5 1.2 %copy-done.8 = bf16[2,512,512]{2,1,0:T(8,128)(2,1)S(1)} copy-done((bf16[2,512,512]{2,1,0:T(8,128)(2,1)S(1)}, bf16[2,512,512]{2,1,0:T(8,128)(2,1)}, u32[]{:S(2)}) %copy-start.8) | copy-done | bytes 1048600
  94.7 1.2 %copy-done.10 = bf16[2,512,512]{2,1,0:T(8,128)(2,1)S(1)} copy-done((bf16[2,512,512]{2,1,0:T(8,128)(2,1)S(1)}, bf16[2,512,512]{2,1,0:T(8,128)(2,1)}, u32[]{:S(2)}) %copy-start.10) | copy-done | bytes 1048600
  96.0 1.2 %copy-done.12 = bf16[2,512,512]{2,1,0:T(8,128)(2,1)S(1)} copy-done((bf16[2,512,512]{2,1,0:T(8,128)(2,1)S(1)}, bf16[2,512,512]{2,1,0:T(8,128)(2,1)}, u32[]{:S(2)}) %copy-start.12) | copy-done | bytes 1048600
  97.2 1.2 %copy-done.14 = bf16[2,512,512]{2,1,0:T(8,128)(2,1)S(1)} copy-done((bf16[2,512,512]{2,1,0:T(8,128)(2,1)S(1)}, bf16[2,512,512]{2,1,0:T(8,128)(2,1)}, u32[]{:S(2)}) %copy-start.14) | copy-done | bytes 1048600
  98.4 1.2 %copy-done.16 = bf16[2,512,512]{2,1,0:T(8,128)(2,1)S(1)} copy-done((bf16[2,512,512]{2,1,0:T(8,128)(2,1)S(1)}, bf16[2,512,512]{2,1,0:T(8,128)(2,1)}, u32[]{:S(2)}) %copy-start.16) | copy-done | bytes 1048600
  99.6 1.2 %copy-done.18 = bf16[2,512,512]{2,1,0:T(8,128)(2,1)S(1)} copy-done((bf16[2,512,512]{2,1,0:T(8,128)(2,1)S(1)}, bf16[2,512,512]{2,1,0:T(8,128)(2,1)}, u32[]{:S(2)}) %copy-start.18) | copy-done | bytes 1048600
  100.9 7.4 %shard_map.61.xy_l = bf16[2,2,512,256]{3,2,1,0:T(8,128)(2,1)S(1)} custom-call(bf16[2,512,512]{2,1,0:T(8,128)(2,1)S(1)} %bitcast.17, bf16[2,512,512]{2,1,0:T(8,128)(2,1)S(1)} %copy-done.8, bf16[2,512,512]{2,1,0:T(8,128)(2,1)S(1)} %copy-done.18, bf16[2,512,512]{2,1,0:T(8,128)(2,1)} %bitcast.1.f.f_r, bf16[2,512,256]{2,1,0:T(8,128)(2,1)} %collective-permute-done.3.g, ...), custom_call_target="tpu_custom_call" | custom-call | flops 5368709120 | bytes 10485760 | tf_op jit(solution)/shard_map/pallas_call | solution.py:137
  108.3 0.0 collective-permute-done.6.ff_r
  108.3 0.0 collective-permute-done.1.ff_l
  108.3 0.0 collective-permute-done.8.xy_r
  108.3 3.8 %shard_map.63 = (f32[2,512,256]{2,1,0:T(8,128)S(1)}, f32[2,512,256]{2,1,0:T(8,128)}) custom-call(s32[1]{0:T(128)} %bitcast.flag, bf16[2,512,512]{2,1,0:T(8,128)(2,1)S(1)} %collective-permute-done.f_l, bf16[2,512,512]{2,1,0:T(8,128)(2,1)} %collective-permute-done.1.ff_l, bf16[2,2,512,256]{3,2,1,0:T(8,128)(2,1)S(1)} %shard_map.61.xy_l, ...), custom_call_target="tpu_custom_call" | custom-call | flops 1073741824 | bytes 10485760 | tf_op jit(solution)/shard_map/pallas_call | solution.py:137
  112.2 0.0 collective-permute-done.10.e
  112.2 0.9 shard_map.64.rest_0_
  113.1 0.0 collective-permute-done.9.e
  113.1 0.7 shard_map.65
  (23 shorter events, 0.0 us)
Async XLA Ops:
  0.6 26.4 %copy-start = (bf16[1,1,2,512,512]{4,3,2,1,0:T(8,128)(2,1)S(1)}, bf16[1,1,2,512,512]{4,3,2,1,0:T(8,128)(2,1)}, u32[]{:S(2)}) copy-start(bf16[1,1,2,512,512]{4,3,2,1,0:T(8,128)(2,1)} %param.4) | copy-start | bytes 3145732
  0.6 26.4 %collective-permute-start.2 = (bf16[2,512,512]{2,1,0:T(8,128)(2,1)}, bf16[2,512,512]{2,1,0:T(8,128)(2,1)S(1)}, u32[]{:S(2)}, u32[]{:S(2)}) collective-permute-start(bf16[2,512,512]{2,1,0:T(8,128)(2,1)} %bitcast.14), channel_id=1, source_target_pairs={{2,0},{6,4},{10,8},{14,12},{18,16},{22,20},{26,24},{30,28},{3,1},{... | collective-permute-start | bytes 3145736 | tf_op jit(solution)/shard_map/ppermute | solution.py:17
  3.3 46.2 %collective-permute-start = (bf16[2,512,512]{2,1,0:T(8,128)(2,1)}, bf16[2,512,512]{2,1,0:T(8,128)(2,1)S(1)}, u32[]{:S(2)}, u32[]{:S(2)}) collective-permute-start(bf16[2,512,512]{2,1,0:T(8,128)(2,1)} %bitcast.1.f.f_r), channel_id=1, source_target_pairs={{2,0},{6,4},{10,8},{14,12},{18,16},{22,20},{26,24},{30,28},{3,1},{... | collective-permute-start | bytes 3145736 | tf_op jit(solution)/shard_map/ppermute | solution.py:17
  27.1 10.4 %copy-start.6 = (bf16[2,512,512]{2,1,0:T(8,128)(2,1)}, bf16[2,512,512]{2,1,0:T(8,128)(2,1)S(1)}, u32[]{:S(2)}) copy-start(bf16[2,512,512]{2,1,0:T(8,128)(2,1)S(1)} %collective-permute-done.2.hr) | copy-start | bytes 3145732
  27.1 1.6 %copy-start.1 = (bf16[1,1,2,512,512]{4,3,2,1,0:T(8,128)(2,1)S(1)}, bf16[1,1,2,512,512]{4,3,2,1,0:T(8,128)(2,1)}, u32[]{:S(2)}) copy-start(bf16[1,1,2,512,512]{4,3,2,1,0:T(8,128)(2,1)} %param.6) | copy-start | bytes 3145732
  28.7 0.7 copy-start.2
  29.4 1.2 %copy-start.3 = (bf16[1,1,2,512,512]{4,3,2,1,0:T(8,128)(2,1)S(1)}, bf16[1,1,2,512,512]{4,3,2,1,0:T(8,128)(2,1)}, u32[]{:S(2)}) copy-start(bf16[1,1,2,512,512]{4,3,2,1,0:T(8,128)(2,1)} %param.7) | copy-start | bytes 3145732
  37.5 22.1 %copy-start.9 = (bf16[2,512,512]{2,1,0:T(8,128)(2,1)}, bf16[2,512,512]{2,1,0:T(8,128)(2,1)S(1)}, u32[]{:S(2)}) copy-start(bf16[2,512,512]{2,1,0:T(8,128)(2,1)S(1)} %get-tuple-element.9.s) | copy-start | bytes 3145732
  37.5 22.1 %copy-start.17 = (bf16[2,512,512]{2,1,0:T(8,128)(2,1)}, bf16[2,512,512]{2,1,0:T(8,128)(2,1)S(1)}, u32[]{:S(2)}) copy-start(bf16[2,512,512]{2,1,0:T(8,128)(2,1)S(1)} %get-tuple-element.7.p) | copy-start | bytes 3145732
  37.5 12.1 %collective-permute-start.4 = (bf16[2,512,512]{2,1,0:T(8,128)(2,1)S(1)}, bf16[2,512,512]{2,1,0:T(8,128)(2,1)S(1)}, u32[]{:S(2)}, u32[]{:S(2)}) collective-permute-start(bf16[2,512,512]{2,1,0:T(8,128)(2,1)S(1)} %get-tuple-element.8.d), channel_id=1, source_target_pairs={{0,1},{1,0},{2,3},{3,2},{4,5},{5,4},{6,7},{7,6},{8,9},{9,8},{10,11... | collective-permute-start | bytes 3145736 | tf_op jit(solution)/shard_map/ppermute | solution.py:21
  37.6 22.0 %collective-permute-start.5 = (bf16[2,512,512]{2,1,0:T(8,128)(2,1)S(1)}, bf16[2,512,512]{2,1,0:T(8,128)(2,1)S(1)}, u32[]{:S(2)}, u32[]{:S(2)}) collective-permute-start(bf16[2,512,512]{2,1,0:T(8,128)(2,1)S(1)} %get-tuple-element.9.s), channel_id=1, source_target_pairs={{0,1},{1,0},{2,3},{3,2},{4,5},{5,4},{6,7},{7,6},{8,9},{9,8},{10,11... | collective-permute-start | bytes 3145736 | tf_op jit(solution)/shard_map/ppermute | solution.py:21
  39.0 20.6 %copy-start.4 = (bf16[1,1,2,512,512]{4,3,2,1,0:T(8,128)(2,1)S(1)}, bf16[1,1,2,512,512]{4,3,2,1,0:T(8,128)(2,1)}, u32[]{:S(2)}) copy-start(bf16[1,1,2,512,512]{4,3,2,1,0:T(8,128)(2,1)} %param.7) | copy-start | bytes 3145732
  39.0 20.6 %copy-start.7 = (bf16[2,512,512]{2,1,0:T(8,128)(2,1)S(1)}, bf16[2,512,512]{2,1,0:T(8,128)(2,1)}, u32[]{:S(2)}) copy-start(bf16[2,512,512]{2,1,0:T(8,128)(2,1)} %copy-done.6) | copy-start | bytes 3145732
  39.0 20.6 %collective-permute-start.7 = (bf16[2,512,256]{2,1,0:T(8,128)(2,1)S(1)}, bf16[2,512,256]{2,1,0:T(8,128)(2,1)S(1)}, u32[]{:S(2)}, u32[]{:S(2)}) collective-permute-start(bf16[2,512,256]{2,1,0:T(8,128)(2,1)S(1)} %get-tuple-element.12), channel_id=1, source_target_pairs={{2,0},{6,4},{10,8},{14,12},{18,16},{22,20},{26,24},{30,28},{3,1},{... | collective-permute-start | bytes 1572872 | tf_op jit(solution)/shard_map/ppermute | solution.py:17
  43.4 64.9 %collective-permute-start.6 = (bf16[2,512,512]{2,1,0:T(8,128)(2,1)}, bf16[2,512,512]{2,1,0:T(8,128)(2,1)S(1)}, u32[]{:S(2)}, u32[]{:S(2)}) collective-permute-start(bf16[2,512,512]{2,1,0:T(8,128)(2,1)} %bitcast.1.f.f_r), channel_id=1, source_target_pairs={{0,1},{1,0},{2,3},{3,2},{4,5},{5,4},{6,7},{7,6},{8,9},{9,8},{10,11... | collective-permute-start | bytes 3145736 | tf_op jit(solution)/shard_map/ppermute | solution.py:21
  49.5 58.8 %collective-permute-start.1 = (bf16[2,512,512]{2,1,0:T(8,128)(2,1)S(1)}, bf16[2,512,512]{2,1,0:T(8,128)(2,1)}, u32[]{:S(2)}, u32[]{:S(2)}) collective-permute-start(bf16[2,512,512]{2,1,0:T(8,128)(2,1)S(1)} %collective-permute-done.f_l), channel_id=1, source_target_pairs={{0,1},{1,0},{2,3},{3,2},{4,5},{5,4},{6,7},{7,6},{8,9},{9,8},{10,11... | collective-permute-start | bytes 3145736 | tf_op jit(solution)/shard_map/ppermute | solution.py:21
  49.5 10.0 %copy-start.11 = (bf16[2,512,512]{2,1,0:T(8,128)(2,1)}, bf16[2,512,512]{2,1,0:T(8,128)(2,1)S(1)}, u32[]{:S(2)}) copy-start(bf16[2,512,512]{2,1,0:T(8,128)(2,1)S(1)} %collective-permute-done.4.df) | copy-start | bytes 3145732
  50.8 17.5 %copy-start.15 = (bf16[2,512,512]{2,1,0:T(8,128)(2,1)}, bf16[2,512,512]{2,1,0:T(8,128)(2,1)S(1)}, u32[]{:S(2)}) copy-start(bf16[2,512,512]{2,1,0:T(8,128)(2,1)S(1)} %shard_map.60.q) | copy-start | bytes 3145732
  59.5 8.7 %copy-start.13 = (bf16[2,512,512]{2,1,0:T(8,128)(2,1)}, bf16[2,512,512]{2,1,0:T(8,128)(2,1)S(1)}, u32[]{:S(2)}) copy-start(bf16[2,512,512]{2,1,0:T(8,128)(2,1)S(1)} %collective-permute-done.5.sf) | copy-start | bytes 3145732
  68.3 40.1 %collective-permute-start.8 = (bf16[2,2,512,256]{3,2,1,0:T(8,128)(2,1)}, bf16[2,2,512,256]{3,2,1,0:T(8,128)(2,1)}, u32[]{:S(2)}, u32[]{:S(2)}) collective-permute-start(bf16[2,2,512,256]{3,2,1,0:T(8,128)(2,1)} %shard_map.62), channel_id=1, source_target_pairs={{0,2},{4,6},{8,10},{12,14},{16,18},{20,22},{24,26},{28,30},{1,3},{... | collective-permute-start | bytes 3145736 | tf_op jit(solution)/shard_map/ppermute | solution.py:17
  69.6 18.1 %collective-permute-start.3 = (bf16[2,512,256]{2,1,0:T(8,128)(2,1)}, bf16[2,512,256]{2,1,0:T(8,128)(2,1)}, u32[]{:S(2)}, u32[]{:S(2)}) collective-permute-start(bf16[2,512,256]{2,1,0:T(8,128)(2,1)} %get-tuple-element.13), channel_id=1, source_target_pairs={{2,0},{6,4},{10,8},{14,12},{18,16},{22,20},{26,24},{30,28},{3,1},{... | collective-permute-start | bytes 1572872 | tf_op jit(solution)/shard_map/ppermute | solution.py:17
  76.8 35.4 %collective-permute-start.10 = (bf16[2,384,256]{2,1,0:T(8,128)(2,1)}, bf16[2,384,256]{2,1,0:T(8,128)(2,1)S(1)}, u32[]{:S(2)}, u32[]{:S(2)}) collective-permute-start(bf16[2,384,256]{2,1,0:T(8,128)(2,1)} %slice.19), channel_id=1, source_target_pairs={{2,0},{6,4},{10,8},{14,12},{18,16},{22,20},{26,24},{30,28},{3,1},{... | collective-permute-start | bytes 1179656 | tf_op jit(solution)/shard_map/ppermute | solution.py:17
  87.7 25.4 %collective-permute-start.9 = (bf16[2,128,256]{2,1,0:T(8,128)(2,1)}, bf16[2,128,256]{2,1,0:T(8,128)(2,1)S(1)}, u32[]{:S(2)}, u32[]{:S(2)}) collective-permute-start(bf16[2,128,256]{2,1,0:T(8,128)(2,1)} %slice.18), channel_id=1, source_target_pairs={{2,0},{6,4},{10,8},{14,12},{18,16},{22,20},{26,24},{30,28},{3,1},{... | collective-permute-start | bytes 393224 | tf_op jit(solution)/shard_map/ppermute | solution.py:17
  92.3 1.2 %copy-start.5 = (bf16[1,1,2,512,512]{4,3,2,1,0:T(8,128)(2,1)S(1)}, bf16[1,1,2,512,512]{4,3,2,1,0:T(8,128)(2,1)}, u32[]{:S(2)}) copy-start(bf16[1,1,2,512,512]{4,3,2,1,0:T(8,128)(2,1)} %param.7) | copy-start | bytes 3145732
  93.5 1.2 %copy-start.8 = (bf16[2,512,512]{2,1,0:T(8,128)(2,1)S(1)}, bf16[2,512,512]{2,1,0:T(8,128)(2,1)}, u32[]{:S(2)}) copy-start(bf16[2,512,512]{2,1,0:T(8,128)(2,1)} %copy-done.6) | copy-start | bytes 3145732
  94.7 1.2 %copy-start.10 = (bf16[2,512,512]{2,1,0:T(8,128)(2,1)S(1)}, bf16[2,512,512]{2,1,0:T(8,128)(2,1)}, u32[]{:S(2)}) copy-start(bf16[2,512,512]{2,1,0:T(8,128)(2,1)} %copy-done.9) | copy-start | bytes 3145732
  96.0 1.2 %copy-start.12 = (bf16[2,512,512]{2,1,0:T(8,128)(2,1)S(1)}, bf16[2,512,512]{2,1,0:T(8,128)(2,1)}, u32[]{:S(2)}) copy-start(bf16[2,512,512]{2,1,0:T(8,128)(2,1)} %copy-done.11) | copy-start | bytes 3145732
  97.2 1.2 %copy-start.14 = (bf16[2,512,512]{2,1,0:T(8,128)(2,1)S(1)}, bf16[2,512,512]{2,1,0:T(8,128)(2,1)}, u32[]{:S(2)}) copy-start(bf16[2,512,512]{2,1,0:T(8,128)(2,1)} %copy-done.13) | copy-start | bytes 3145732
  98.4 1.2 %copy-start.16 = (bf16[2,512,512]{2,1,0:T(8,128)(2,1)S(1)}, bf16[2,512,512]{2,1,0:T(8,128)(2,1)}, u32[]{:S(2)}) copy-start(bf16[2,512,512]{2,1,0:T(8,128)(2,1)} %copy-done.15) | copy-start | bytes 3145732
  99.6 1.2 %copy-start.18 = (bf16[2,512,512]{2,1,0:T(8,128)(2,1)S(1)}, bf16[2,512,512]{2,1,0:T(8,128)(2,1)}, u32[]{:S(2)}) copy-start(bf16[2,512,512]{2,1,0:T(8,128)(2,1)} %copy-done.17) | copy-start | bytes 3145732
where the time goes:
time: 115 us; the launch traced here: 114 us
  waiting for transfers between devices  44.9 us (39%)
  Pallas kernels  31 us (27%)
  starting transfers between devices  22.6 us (20%)
  local copies, waits for them, and re-layouts  14.5 us (13%)
    ppermute x7, waiting for transfers between devices, across(): lax.ppermute(x, axis, [(i, i ^ 1) for i in range(lax.axis_size(axis)) if...  44.9 us
    pallas_call x7, Pallas kernels, call(): pl.pallas_call(body, out_shape=[jax.ShapeDtypeStruct(s, t) for s, t in ou...  29.7 us
    ppermute x7, starting transfers between devices, across(): lax.ppermute(x, axis, [(i, i ^ 1) for i in range(lax.axis_size(axis)) if...  21.9 us
    unnamed x38, local copies, waits for them, and re-layouts  12.1 us
  transfers between devices with their start and end apart: 11, of which 4 were waited for; matrix products, arithmetic and copies ran while one was open for 2% of the time, Pallas kernels for 27%

commit v1 on v0

--- a/solution.py
+++ b/solution.py
@@ -88,35 +88,48 @@
     cstage(sf, w, plain(xy.at[1]))
 
 
-def last(factor, flag, f_l, ff_l, xy_l, f_r, ff_r, xy_r, e_r, own, far, f, ff, xy, e, sems):
-    def fetch(sources):
-        copies = [pltpu.make_async_copy(a, b, sems.at[i]) for i, (a, b) in enumerate(sources)]
+def fetch(flag, left, right, sems):
+    def run(pairs):
+        copies = [pltpu.make_async_copy(a, b, sems.at[i]) for i, (a, b) in enumerate(pairs)]
         for c in copies:
             c.start()
         for c in copies:
             c.wait()
 
-    half = e.shape[2]
-
     @pl.when(flag[0] == 1)
     def _():
-        fetch([(f_l, f), (ff_l, ff), (xy_l, xy)])
-        e[...] = jnp.zeros_like(e)
+        run(left)
 
     @pl.when(flag[0] == 0)
     def _():
-        fetch([(f_r, f), (ff_r, ff), (xy_r, xy), (e_r.at[:, :, pl.ds(half, half)], e)])
-
-    def scaled(dst, base=None):
-        def emit(re, im):
-            if base is not None:
-                re, im = base[0].astype(F32) + re, base[1].astype(F32) + im
-            dst[0], dst[1] = re * factor, im * factor
-
-        return emit
-
-    cstage(f, xy.at[0], scaled(own, e))
-    cstage(ff, xy.at[1], scaled(far))
+        run(right)
+
+
+def last_own(factor, flag, f_l, xy_l, f_r, xy_r, e_r, own, f, x, e, sems):
+    half = e.shape[2]
+    e[...] = jnp.zeros_like(e)
+    fetch(
+        flag,
+        [(f_l, f), (xy_l.at[0], x)],
+        [(f_r, f), (xy_r.at[0], x), (e_r.at[:, :, pl.ds(half, half)], e)],
+        sems,
+    )
+
+    def emit(re, im):
+        own[0] = (e[0].astype(F32) + re) * factor
+        own[1] = (e[1].astype(F32) + im) * factor
+
+    cstage(f, x, emit)
+
+
+def last_far(factor, flag, f_l, xy_l, f_r, xy_r, far, f, y, sems):
+    fetch(flag, [(f_l, f), (xy_l.at[1], y)], [(f_r, f), (xy_r.at[1], y)], sems)
+
+    def emit(re, im):
+        far[0] = re * factor
+        far[1] = im * factor
+
+    cstage(f, y, emit)
 
 
 def finish(factor, first, own, e, *rest):
@@ -132,7 +145,7 @@
 
 
 def call(body, outs, args, units, scratch=(), specs=None, out_spec=None, aliases=None):
-    n = args[-1].shape[1] if units else 0
+    n = args[1].shape[1]
     vmem = pl.BlockSpec(memory_space=pltpu.VMEM)
     return pl.pallas_call(
         body,
@@ -145,7 +158,7 @@
             bytes_accessed=4 * n * n * (len(args) + len(outs)),
             transcendentals=0,
         ),
-        compiler_params=pltpu.CompilerParams(vmem_limit_bytes=24 << 20),
+        compiler_params=pltpu.CompilerParams(vmem_limit_bytes=14 << 20),
         input_output_aliases=aliases or {},
     )(*args)
 
@@ -161,9 +174,8 @@
     inflow_r1 = across(inflow[:, :, half:], "long", 1)
     inflow_r0 = across(inflow[:, :, :half], "long", 1)
     outflow_r = across(outflow, "long", 1)
-    cut = n * 3 // 4
-    outer_r0 = across(outer[:, :cut, :half], "long", 1)
-    outer_r1 = across(outer[:, cut:, :half], "long", 1)
+    cuts = [n * c // 16 for c in [0, 8, 12, 16]]
+    outer_rs = [across(outer[:, a:b, :half], "long", 1) for a, b in zip(cuts, cuts[1:])]
     outflow_far = swap(outflow, "short")
 
     token = pl.pallas_call(
@@ -197,13 +209,22 @@
     outflow_r_far = swap(outflow_r, "short")
     flag = (lax.axis_index("long") % 2 == 0).astype(jnp.int32).reshape(1)
     hbm = pl.BlockSpec(memory_space=pltpu.HBM)
-    own, far = call(
-        functools.partial(last, factor),
-        [(part, F32)] * 2,
-        (flag, outflow_r, outflow_r_far, xy0, outflow, outflow_far, xy1_r, outer),
-        1,
-        [(full, BF), (full, BF), ((2,) + part, BF), (part, BF), pltpu.SemaphoreType.DMA((4,))],
-        [pl.BlockSpec(memory_space=pltpu.SMEM)] + [hbm] * 7,
+    smem = pl.BlockSpec(memory_space=pltpu.SMEM)
+    (own,) = call(
+        functools.partial(last_own, factor),
+        [(part, F32)],
+        (flag, outflow_r, xy0, outflow, xy1_r, outer),
+        0.5,
+        [(full, BF), (part, BF), (part, BF), pltpu.SemaphoreType.DMA((3,))],
+        [smem] + [hbm] * 5,
+    )
+    (far,) = call(
+        functools.partial(last_far, factor),
+        [(part, F32)],
+        (flag, outflow_r_far, xy0, outflow_far, xy1_r),
+        0.5,
+        [(full, BF), (part, BF), pltpu.SemaphoreType.DMA((2,))],
+        [smem] + [hbm] * 4,
     )
 
     def add(first, rows, *more):
@@ -218,8 +239,10 @@
             {2: 0} if more else None,
         )[0]
 
-    partly = add(0, (outer_r0,))
-    own = add(cut, (outer_r1,), partly)
+    total = ()
+    for i, piece in enumerate(outer_rs):
+        total = (add(cuts[i], (piece,), *total),)
+    own = total[0]
     return own[None], far[None]
 
 

time: 115 us -> 118 us (1.026)
  the two profiles are of different devices: /device:TPU:6 before, /device:TPU:0 now
where the time goes in v1:
time: 118 us; the launch traced here: 117 us
  waiting for transfers between devices  59.5 us (50%)
  Pallas kernels  29.8 us (25%)
  local copies, waits for them, and re-layouts  15 us (13%)
  starting transfers between devices  11.6 us (10%)
    ppermute x8, waiting for transfers between devices, across(): lax.ppermute(x, axis, [(i, i ^ 1) for i in range(lax.axis_size(axis)) if...  59.5 us
    pallas_call x9, Pallas kernels, call(): pl.pallas_call(body, out_shape=[jax.ShapeDtypeStruct(s, t) for s, t in ou...  28.5 us
    unnamed x42, local copies, waits for them, and re-layouts  13.3 us
    ppermute x8, starting transfers between devices, across(): lax.ppermute(x, axis, [(i, i ^ 1) for i in range(lax.axis_size(axis)) if...  11 us
  transfers between devices with their start and end apart: 12, of which 4 were waited for; matrix products, arithmetic and copies ran while one was open for 1% of the time, Pallas kernels for 20%

profile of v1, /device:TPU:0, one launch (start us, length us, event | category | flops | bytes accessed | tf_op | source)
XLA Modules:
  0.0 117.0 jit_solution(13303902224696152644)
XLA Ops:
  0.6 1.4 %collective-permute-start.1 = (bf16[2,512,512]{2,1,0:T(8,128)(2,1)}, bf16[2,512,512]{2,1,0:T(8,128)(2,1)S(1)}, u32[]{:S(2)}, u32[]{:S(2)}) collective-permute-start(bf16[2,512,512]{2,1,0:T(8,128)(2,1)} %bitcast.20), channel_id=1, source_target_pairs={{2,0},{6,4},{10,8},{14,12},{18,16},{22,20},{26,24},{30,28},{3,1},{... | collective-permute-start | bytes 3145736 | tf_op jit(solution)/shard_map/ppermute | solution.py:17
  2.1 1.3 %gate.1.t = bf16[1,16,128]{2,1,0:T(8,128)(2,1)} custom-call(bf16[2,512,512]{2,1,0:T(8,128)(2,1)} %bitcast.7), custom_call_target="tpu_custom_call" | custom-call | tf_op jit(solution)/shard_map/gate/pallas_call | solution.py:181
  3.4 25.1 %collective-permute-done.1.hr = bf16[2,512,512]{2,1,0:T(8,128)(2,1)S(1)} collective-permute-done((bf16[2,512,512]{2,1,0:T(8,128)(2,1)}, bf16[2,512,512]{2,1,0:T(8,128)(2,1)S(1)}, u32[]{:S(2)}, u32[]{:S(2)}) %collective-permute-start.1) | collective-permute-done | bytes 1048608 | tf_op jit(solution)/shard_map/ppermute | solution.py:17
  28.4 1.6 %copy-done.1 = bf16[1,1,2,512,512]{4,3,2,1,0:T(8,128)(2,1)S(1)} copy-done((bf16[1,1,2,512,512]{4,3,2,1,0:T(8,128)(2,1)S(1)}, bf16[1,1,2,512,512]{4,3,2,1,0:T(8,128)(2,1)}, u32[]{:S(2)}) %copy-start.1) | copy-done | bytes 1048600
  30.0 1.2 %copy-done.3 = bf16[1,1,2,512,512]{4,3,2,1,0:T(8,128)(2,1)S(1)} copy-done((bf16[1,1,2,512,512]{4,3,2,1,0:T(8,128)(2,1)S(1)}, bf16[1,1,2,512,512]{4,3,2,1,0:T(8,128)(2,1)}, u32[]{:S(2)}) %copy-start.3) | copy-done | bytes 1048600
  31.3 0.7 copy-done.4
  32.0 1.2 %copy-done.5 = bf16[1,1,2,512,512]{4,3,2,1,0:T(8,128)(2,1)S(1)} copy-done((bf16[1,1,2,512,512]{4,3,2,1,0:T(8,128)(2,1)S(1)}, bf16[1,1,2,512,512]{4,3,2,1,0:T(8,128)(2,1)}, u32[]{:S(2)}) %copy-start.5) | copy-done | bytes 1048600
  33.2 5.6 %shard_map.59 = (bf16[2,512,512]{2,1,0:T(8,128)(2,1)S(1)}, bf16[2,512,512]{2,1,0:T(8,128)(2,1)S(1)}, bf16[2,512,512]{2,1,0:T(8,128)(2,1)S(1)}) custom-call(bf16[1,16,128]{2,1,0:T(8,128)(2,1)S(1)} %copy-done.4, bf16[2,512,512]{2,1,0:T(8,128)(2,1)S(1)} %bitcast.21, bf16[2,512,512]{2,1,0:T(8,128)(2,1)S(1)} %collective-permute-done.1.hr, ...), custom_call_target="tpu_custom_call" | custom-call | flops 5368709120 | bytes 9437184 | tf_op jit(solution)/shard_map/pallas_call | solution.py:150
  38.9 0.0 copy-start.19
  38.9 0.1 collective-permute-start.3
  38.9 0.0 copy-start.2
  39.0 0.5 collective-permute-start.4
  39.4 0.9 fusion.1
  40.4 1.4 %collective-permute-start.5 = (bf16[2,512,256]{2,1,0:T(8,128)(2,1)S(1)}, bf16[2,512,256]{2,1,0:T(8,128)(2,1)S(1)}, u32[]{:S(2)}, u32[]{:S(2)}) collective-permute-start(bf16[2,512,256]{2,1,0:T(8,128)(2,1)S(1)} %get-tuple-element.10), channel_id=1, source_target_pairs={{2,0},{6,4},{10,8},{14,12},{18,16},{22,20},{26,24},{30,28},{3,1},{... | collective-permute-start | bytes 1572872 | tf_op jit(solution)/shard_map/ppermute | solution.py:17
  41.8 1.3 %collective-permute-start = (bf16[2,512,512]{2,1,0:T(8,128)(2,1)S(1)}, bf16[2,512,512]{2,1,0:T(8,128)(2,1)}, u32[]{:S(2)}, u32[]{:S(2)}) collective-permute-start(bf16[2,512,512]{2,1,0:T(8,128)(2,1)S(1)} %bitcast.13), channel_id=1, source_target_pairs={{2,0},{6,4},{10,8},{14,12},{18,16},{22,20},{26,24},{30,28},{3,1},{... | collective-permute-start | bytes 3145736 | tf_op jit(solution)/shard_map/ppermute | solution.py:17
  43.1 0.0 collective-permute-done.3.df
  43.1 1.2 %shard_map.60.q = bf16[2,512,512]{2,1,0:T(8,128)(2,1)S(1)} custom-call(bf16[2,512,512]{2,1,0:T(8,128)(2,1)S(1)} %get-tuple-element.6.d, bf16[2,512,512]{2,1,0:T(8,128)(2,1)S(1)} %collective-permute-done.3.df), custom_call_target="tpu_custom_call" | custom-call | flops 1073741824 | bytes 3145728 | tf_op jit(solution)/shard_map/pallas_call | solution.py:150
  44.4 12.8 %collective-permute-done.5.g = bf16[2,512,256]{2,1,0:T(8,128)(2,1)S(1)} collective-permute-done((bf16[2,512,256]{2,1,0:T(8,128)(2,1)S(1)}, bf16[2,512,256]{2,1,0:T(8,128)(2,1)S(1)}, u32[]{:S(2)}, u32[]{:S(2)}) %collective-permute-start.5) | collective-permute-done | bytes 524320 | tf_op jit(solution)/shard_map/ppermute | solution.py:17
  57.2 0.0 collective-permute-done.4.sf
  57.2 7.2 %shard_map.62 = bf16[2,2,512,256]{3,2,1,0:T(8,128)(2,1)} custom-call(bf16[2,512,512]{2,1,0:T(8,128)(2,1)S(1)} %bitcast.22, bf16[2,512,512]{2,1,0:T(8,128)(2,1)S(1)} %copy-done.9, bf16[2,512,512]{2,1,0:T(8,128)(2,1)S(1)} %get-tuple-element.5.p, bf16[2,512,512]{2,1,0:T(8,128)(2,1)S(1)} %bitcast.14, bf16[2,512,256]{2,1,0:T(8,128)(2,1)S(1)} %collective-permute-done.5.g, ...), custom_call_target="tpu_custom_call" | custom-call | flops 5368709120 | bytes 10485760 | tf_op jit(solution)/shard_map/pallas_call | solution.py:150
  64.4 1.5 %collective-permute-start.6 = (bf16[2,2,512,256]{3,2,1,0:T(8,128)(2,1)}, bf16[2,2,512,256]{3,2,1,0:T(8,128)(2,1)S(1)}, u32[]{:S(2)}, u32[]{:S(2)}) collective-permute-start(bf16[2,2,512,256]{3,2,1,0:T(8,128)(2,1)} %shard_map.62), channel_id=1, source_target_pairs={{0,2},{4,6},{8,10},{12,14},{16,18},{20,22},{24,26},{28,30},{1,3},{... | collective-permute-start | bytes 3145736 | tf_op jit(solution)/shard_map/ppermute | solution.py:17
  65.9 1.3 %collective-permute-start.2 = (bf16[2,512,256]{2,1,0:T(8,128)(2,1)}, bf16[2,512,256]{2,1,0:T(8,128)(2,1)}, u32[]{:S(2)}, u32[]{:S(2)}) collective-permute-start(bf16[2,512,256]{2,1,0:T(8,128)(2,1)} %get-tuple-element.11), channel_id=1, source_target_pairs={{2,0},{6,4},{10,8},{14,12},{18,16},{22,20},{26,24},{30,28},{3,1},{... | collective-permute-start | bytes 1572872 | tf_op jit(solution)/shard_map/ppermute | solution.py:17
  67.2 0.1 collective-permute-start.11
  67.3 12.4 %collective-permute-done.f_l = bf16[2,512,512]{2,1,0:T(8,128)(2,1)} collective-permute-done((bf16[2,512,512]{2,1,0:T(8,128)(2,1)S(1)}, bf16[2,512,512]{2,1,0:T(8,128)(2,1)}, u32[]{:S(2)}, u32[]{:S(2)}) %collective-permute-start) | collective-permute-done | bytes 1048608 | tf_op jit(solution)/shard_map/ppermute | solution.py:17
  79.7 0.0 collective-permute-start.10
  79.7 0.7 slice.24
  80.5 1.3 %collective-permute-start.9 = (bf16[2,256,256]{2,1,0:T(8,128)(2,1)}, bf16[2,256,256]{2,1,0:T(8,128)(2,1)S(1)}, u32[]{:S(2)}, u32[]{:S(2)}) collective-permute-start(bf16[2,256,256]{2,1,0:T(8,128)(2,1)} %slice.24), channel_id=1, source_target_pairs={{2,0},{6,4},{10,8},{14,12},{18,16},{22,20},{26,24},{30,28},{3,1},{... | collective-permute-start | bytes 786440 | tf_op jit(solution)/shard_map/ppermute | solution.py:17
  81.8 9.2 %collective-permute-done.2.g = bf16[2,512,256]{2,1,0:T(8,128)(2,1)} collective-permute-done((bf16[2,512,256]{2,1,0:T(8,128)(2,1)}, bf16[2,512,256]{2,1,0:T(8,128)(2,1)}, u32[]{:S(2)}, u32[]{:S(2)}) %collective-permute-start.2) | collective-permute-done | bytes 524320 | tf_op jit(solution)/shard_map/ppermute | solution.py:17
  91.0 1.3 %collective-permute-start.8 = (bf16[2,128,256]{2,1,0:T(8,128)(2,1)S(1)}, bf16[2,128,256]{2,1,0:T(8,128)(2,1)S(1)}, u32[]{:S(2)}, u32[]{:S(2)}) collective-permute-start(bf16[2,128,256]{2,1,0:T(8,128)(2,1)S(1)} %get-tuple-element.8), channel_id=1, source_target_pairs={{2,0},{6,4},{10,8},{14,12},{18,16},{22,20},{26,24},{30,28},{3,1},{... | collective-permute-start | bytes 393224 | tf_op jit(solution)/shard_map/ppermute | solution.py:17
  92.3 0.0 collective-permute-done.6.xy_r
  92.3 1.5 %collective-permute-start.7 = (bf16[2,128,256]{2,1,0:T(8,128)(2,1)S(1)}, bf16[2,128,256]{2,1,0:T(8,128)(2,1)S(1)}, u32[]{:S(2)}, u32[]{:S(2)}) collective-permute-start(bf16[2,128,256]{2,1,0:T(8,128)(2,1)S(1)} %get-tuple-element.9), channel_id=1, source_target_pairs={{2,0},{6,4},{10,8},{14,12},{18,16},{22,20},{26,24},{30,28},{3,1},{... | collective-permute-start | bytes 393224 | tf_op jit(solution)/shard_map/ppermute | solution.py:17
  93.8 0.0 copy-start.7
  93.8 1.2 %copy-done.7 = bf16[1,1,2,512,512]{4,3,2,1,0:T(8,128)(2,1)S(1)} copy-done((bf16[1,1,2,512,512]{4,3,2,1,0:T(8,128)(2,1)S(1)}, bf16[1,1,2,512,512]{4,3,2,1,0:T(8,128)(2,1)}, u32[]{:S(2)}) %copy-start.7) | copy-done | bytes 1048600
  95.0 1.2 %copy-done.10 = bf16[2,512,512]{2,1,0:T(8,128)(2,1)S(1)} copy-done((bf16[2,512,512]{2,1,0:T(8,128)(2,1)S(1)}, bf16[2,512,512]{2,1,0:T(8,128)(2,1)}, u32[]{:S(2)}) %copy-start.10) | copy-done | bytes 1048600
  96.2 1.2 %copy-done.12 = bf16[2,512,512]{2,1,0:T(8,128)(2,1)S(1)} copy-done((bf16[2,512,512]{2,1,0:T(8,128)(2,1)S(1)}, bf16[2,512,512]{2,1,0:T(8,128)(2,1)}, u32[]{:S(2)}) %copy-start.12) | copy-done | bytes 1048600
  97.4 1.2 %copy-done.14 = bf16[2,512,512]{2,1,0:T(8,128)(2,1)S(1)} copy-done((bf16[2,512,512]{2,1,0:T(8,128)(2,1)S(1)}, bf16[2,512,512]{2,1,0:T(8,128)(2,1)}, u32[]{:S(2)}) %copy-start.14) | copy-done | bytes 1048600
  98.7 1.2 %copy-done.16 = bf16[2,512,512]{2,1,0:T(8,128)(2,1)S(1)} copy-done((bf16[2,512,512]{2,1,0:T(8,128)(2,1)S(1)}, bf16[2,512,512]{2,1,0:T(8,128)(2,1)}, u32[]{:S(2)}) %copy-start.16) | copy-done | bytes 1048600
  99.9 1.2 %copy-done.18 = bf16[2,512,512]{2,1,0:T(8,128)(2,1)S(1)} copy-done((bf16[2,512,512]{2,1,0:T(8,128)(2,1)S(1)}, bf16[2,512,512]{2,1,0:T(8,128)(2,1)}, u32[]{:S(2)}) %copy-start.18) | copy-done | bytes 1048600
  101.1 1.2 %copy-done.20 = bf16[2,512,512]{2,1,0:T(8,128)(2,1)S(1)} copy-done((bf16[2,512,512]{2,1,0:T(8,128)(2,1)S(1)}, bf16[2,512,512]{2,1,0:T(8,128)(2,1)}, u32[]{:S(2)}) %copy-start.20) | copy-done | bytes 1048600
  102.3 7.1 %shard_map.61.xy_l = bf16[2,2,512,256]{3,2,1,0:T(8,128)(2,1)S(1)} custom-call(bf16[2,512,512]{2,1,0:T(8,128)(2,1)S(1)} %bitcast.23, bf16[2,512,512]{2,1,0:T(8,128)(2,1)S(1)} %copy-done.10, bf16[2,512,512]{2,1,0:T(8,128)(2,1)S(1)} %copy-done.20, bf16[2,512,512]{2,1,0:T(8,128)(2,1)S(1)} %bitcast.16, bf16[2,512,256]{2,1,0:T(8,128)(2,1)} %collective-permute-done.2.g, ...), custom_call_target="tpu_custom_call" | custom-call | flops 5368709120 | bytes 10485760 | tf_op jit(solution)/shard_map/pallas_call | solution.py:150
  109.5 2.0 %shard_map.63.own = f32[2,512,256]{2,1,0:T(8,128)S(1)} custom-call(s32[1]{0:T(128)} %bitcast.flag, bf16[2,512,512]{2,1,0:T(8,128)(2,1)} %collective-permute-done.f_l, bf16[2,2,512,256]{3,2,1,0:T(8,128)(2,1)S(1)} %shard_map.61.xy_l, bf16[2,512,512]{2,1,0:T(8,128)(2,1)S(1)} %bitcast.17, bf16[2,2,512,256]{3,2,1,0:T(8,128)(2,1)S(1)} %collective-permute-done.6.xy_r, ...), custom_call_target="tpu_custom_call" | custom-call | flops 536870912 | bytes 7340032 | tf_op jit(solution)/shard_map/pallas_call | solution.py:150
  111.5 0.8 shard_map.64.rest_0_
  112.3 0.0 collective-permute-done.8.e
  112.3 0.7 shard_map.65.rest_0_
  113.1 0.0 collective-permute-done.11.f_r
  113.1 2.9 %shard_map.67 = f32[2,512,256]{2,1,0:T(8,128)} custom-call(s32[1]{0:T(128)} %bitcast.flag, bf16[2,512,512]{2,1,0:T(8,128)(2,1)} %collective-permute-done.10.f_l, bf16[2,2,512,256]{3,2,1,0:T(8,128)(2,1)S(1)} %shard_map.61.xy_l, bf16[2,512,512]{2,1,0:T(8,128)(2,1)} %collective-permute-done.11.f_r, bf16[2,2,512,256]{3,2,1,0:T(8,128)(2,1)S(1)} %collective-permute-done.6.xy_r), custom_call_target="tpu_custom_call" | custom-call | flops 536870912 | bytes 6291456 | tf_op jit(solution)/shard_map/pallas_call | solution.py:150
  116.0 0.0 collective-permute-done.7.e
  116.1 0.7 shard_map.66
  (31 shorter events, 0.1 us)
Async XLA Ops:
  0.6 27.8 %copy-start = (bf16[1,1,2,512,512]{4,3,2,1,0:T(8,128)(2,1)S(1)}, bf16[1,1,2,512,512]{4,3,2,1,0:T(8,128)(2,1)}, u32[]{:S(2)}) copy-start(bf16[1,1,2,512,512]{4,3,2,1,0:T(8,128)(2,1)} %param.4) | copy-start | bytes 3145732
  0.6 27.8 %collective-permute-start.1 = (bf16[2,512,512]{2,1,0:T(8,128)(2,1)}, bf16[2,512,512]{2,1,0:T(8,128)(2,1)S(1)}, u32[]{:S(2)}, u32[]{:S(2)}) collective-permute-start(bf16[2,512,512]{2,1,0:T(8,128)(2,1)} %bitcast.20), channel_id=1, source_target_pairs={{2,0},{6,4},{10,8},{14,12},{18,16},{22,20},{26,24},{30,28},{3,1},{... | collective-permute-start | bytes 3145736 | tf_op jit(solution)/shard_map/ppermute | solution.py:17
  28.4 10.4 %copy-start.8 = (bf16[2,512,512]{2,1,0:T(8,128)(2,1)}, bf16[2,512,512]{2,1,0:T(8,128)(2,1)S(1)}, u32[]{:S(2)}) copy-start(bf16[2,512,512]{2,1,0:T(8,128)(2,1)S(1)} %collective-permute-done.1.hr) | copy-start | bytes 3145732
  28.4 1.6 %copy-start.1 = (bf16[1,1,2,512,512]{4,3,2,1,0:T(8,128)(2,1)S(1)}, bf16[1,1,2,512,512]{4,3,2,1,0:T(8,128)(2,1)}, u32[]{:S(2)}) copy-start(bf16[1,1,2,512,512]{4,3,2,1,0:T(8,128)(2,1)} %param.5) | copy-start | bytes 3145732
  30.0 1.2 %copy-start.3 = (bf16[1,1,2,512,512]{4,3,2,1,0:T(8,128)(2,1)S(1)}, bf16[1,1,2,512,512]{4,3,2,1,0:T(8,128)(2,1)}, u32[]{:S(2)}) copy-start(bf16[1,1,2,512,512]{4,3,2,1,0:T(8,128)(2,1)} %param.6) | copy-start | bytes 3145732
  31.3 0.7 copy-start.4
  32.0 1.2 %copy-start.5 = (bf16[1,1,2,512,512]{4,3,2,1,0:T(8,128)(2,1)S(1)}, bf16[1,1,2,512,512]{4,3,2,1,0:T(8,128)(2,1)}, u32[]{:S(2)}) copy-start(bf16[1,1,2,512,512]{4,3,2,1,0:T(8,128)(2,1)} %param.7) | copy-start | bytes 3145732
  38.8 18.3 %copy-start.11 = (bf16[2,512,512]{2,1,0:T(8,128)(2,1)}, bf16[2,512,512]{2,1,0:T(8,128)(2,1)S(1)}, u32[]{:S(2)}) copy-start(bf16[2,512,512]{2,1,0:T(8,128)(2,1)S(1)} %get-tuple-element.7.s) | copy-start | bytes 3145732
  38.9 18.3 %copy-start.19 = (bf16[2,512,512]{2,1,0:T(8,128)(2,1)}, bf16[2,512,512]{2,1,0:T(8,128)(2,1)S(1)}, u32[]{:S(2)}) copy-start(bf16[2,512,512]{2,1,0:T(8,128)(2,1)S(1)} %get-tuple-element.5.p) | copy-start | bytes 3145732
  38.9 4.2 %collective-permute-start.3 = (bf16[2,512,512]{2,1,0:T(8,128)(2,1)S(1)}, bf16[2,512,512]{2,1,0:T(8,128)(2,1)S(1)}, u32[]{:S(2)}, u32[]{:S(2)}) collective-permute-start(bf16[2,512,512]{2,1,0:T(8,128)(2,1)S(1)} %get-tuple-element.6.d), channel_id=1, source_target_pairs={{0,1},{1,0},{2,3},{3,2},{4,5},{5,4},{6,7},{7,6},{8,9},{9,8},{10,11... | collective-permute-start | bytes 3145736 | tf_op jit(solution)/shard_map/ppermute | solution.py:21
  38.9 2.8 %copy-start.2 = (bf16[1,1,2,512,512]{4,3,2,1,0:T(8,128)(2,1)S(1)}, bf16[1,1,2,512,512]{4,3,2,1,0:T(8,128)(2,1)}, u32[]{:S(2)}) copy-start(bf16[1,1,2,512,512]{4,3,2,1,0:T(8,128)(2,1)} %param.5) | copy-start | bytes 3145732
  39.0 18.2 %collective-permute-start.4 = (bf16[2,512,512]{2,1,0:T(8,128)(2,1)S(1)}, bf16[2,512,512]{2,1,0:T(8,128)(2,1)S(1)}, u32[]{:S(2)}, u32[]{:S(2)}) collective-permute-start(bf16[2,512,512]{2,1,0:T(8,128)(2,1)S(1)} %get-tuple-element.7.s), channel_id=1, source_target_pairs={{0,1},{1,0},{2,3},{3,2},{4,5},{5,4},{6,7},{7,6},{8,9},{9,8},{10,11... | collective-permute-start | bytes 3145736 | tf_op jit(solution)/shard_map/ppermute | solution.py:21
  40.4 16.8 %copy-start.6 = (bf16[1,1,2,512,512]{4,3,2,1,0:T(8,128)(2,1)S(1)}, bf16[1,1,2,512,512]{4,3,2,1,0:T(8,128)(2,1)}, u32[]{:S(2)}) copy-start(bf16[1,1,2,512,512]{4,3,2,1,0:T(8,128)(2,1)} %param.7) | copy-start | bytes 3145732
  40.4 16.9 %copy-start.9 = (bf16[2,512,512]{2,1,0:T(8,128)(2,1)S(1)}, bf16[2,512,512]{2,1,0:T(8,128)(2,1)}, u32[]{:S(2)}) copy-start(bf16[2,512,512]{2,1,0:T(8,128)(2,1)} %copy-done.8) | copy-start | bytes 3145732
  40.4 16.8 %collective-permute-start.5 = (bf16[2,512,256]{2,1,0:T(8,128)(2,1)S(1)}, bf16[2,512,256]{2,1,0:T(8,128)(2,1)S(1)}, u32[]{:S(2)}, u32[]{:S(2)}) collective-permute-start(bf16[2,512,256]{2,1,0:T(8,128)(2,1)S(1)} %get-tuple-element.10), channel_id=1, source_target_pairs={{2,0},{6,4},{10,8},{14,12},{18,16},{22,20},{26,24},{30,28},{3,1},{... | collective-permute-start | bytes 1572872 | tf_op jit(solution)/shard_map/ppermute | solution.py:17
  41.8 38.0 %collective-permute-start = (bf16[2,512,512]{2,1,0:T(8,128)(2,1)S(1)}, bf16[2,512,512]{2,1,0:T(8,128)(2,1)}, u32[]{:S(2)}, u32[]{:S(2)}) collective-permute-start(bf16[2,512,512]{2,1,0:T(8,128)(2,1)S(1)} %bitcast.13), channel_id=1, source_target_pairs={{2,0},{6,4},{10,8},{14,12},{18,16},{22,20},{26,24},{30,28},{3,1},{... | collective-permute-start | bytes 3145736 | tf_op jit(solution)/shard_map/ppermute | solution.py:17
  43.1 14.1 %copy-start.13 = (bf16[2,512,512]{2,1,0:T(8,128)(2,1)}, bf16[2,512,512]{2,1,0:T(8,128)(2,1)S(1)}, u32[]{:S(2)}) copy-start(bf16[2,512,512]{2,1,0:T(8,128)(2,1)S(1)} %collective-permute-done.3.df) | copy-start | bytes 3145732
  44.4 20.1 %copy-start.17 = (bf16[2,512,512]{2,1,0:T(8,128)(2,1)}, bf16[2,512,512]{2,1,0:T(8,128)(2,1)S(1)}, u32[]{:S(2)}) copy-start(bf16[2,512,512]{2,1,0:T(8,128)(2,1)S(1)} %shard_map.60.q) | copy-start | bytes 3145732
  57.2 7.3 %copy-start.15 = (bf16[2,512,512]{2,1,0:T(8,128)(2,1)}, bf16[2,512,512]{2,1,0:T(8,128)(2,1)S(1)}, u32[]{:S(2)}) copy-start(bf16[2,512,512]{2,1,0:T(8,128)(2,1)S(1)} %collective-permute-done.4.sf) | copy-start | bytes 3145732
  64.4 27.8 %collective-permute-start.6 = (bf16[2,2,512,256]{3,2,1,0:T(8,128)(2,1)}, bf16[2,2,512,256]{3,2,1,0:T(8,128)(2,1)S(1)}, u32[]{:S(2)}, u32[]{:S(2)}) collective-permute-start(bf16[2,2,512,256]{3,2,1,0:T(8,128)(2,1)} %shard_map.62), channel_id=1, source_target_pairs={{0,2},{4,6},{8,10},{12,14},{16,18},{20,22},{24,26},{28,30},{1,3},{... | collective-permute-start | bytes 3145736 | tf_op jit(solution)/shard_map/ppermute | solution.py:17
  65.9 25.0 %collective-permute-start.2 = (bf16[2,512,256]{2,1,0:T(8,128)(2,1)}, bf16[2,512,256]{2,1,0:T(8,128)(2,1)}, u32[]{:S(2)}, u32[]{:S(2)}) collective-permute-start(bf16[2,512,256]{2,1,0:T(8,128)(2,1)} %get-tuple-element.11), channel_id=1, source_target_pairs={{2,0},{6,4},{10,8},{14,12},{18,16},{22,20},{26,24},{30,28},{3,1},{... | collective-permute-start | bytes 1572872 | tf_op jit(solution)/shard_map/ppermute | solution.py:17
  67.2 45.8 %collective-permute-start.11 = (bf16[2,512,512]{2,1,0:T(8,128)(2,1)S(1)}, bf16[2,512,512]{2,1,0:T(8,128)(2,1)}, u32[]{:S(2)}, u32[]{:S(2)}) collective-permute-start(bf16[2,512,512]{2,1,0:T(8,128)(2,1)S(1)} %bitcast.15), channel_id=1, source_target_pairs={{0,1},{1,0},{2,3},{3,2},{4,5},{5,4},{6,7},{7,6},{8,9},{9,8},{10,11... | collective-permute-start | bytes 3145736 | tf_op jit(solution)/shard_map/ppermute | solution.py:21
  79.7 33.3 %collective-permute-start.10 = (bf16[2,512,512]{2,1,0:T(8,128)(2,1)}, bf16[2,512,512]{2,1,0:T(8,128)(2,1)}, u32[]{:S(2)}, u32[]{:S(2)}) collective-permute-start(bf16[2,512,512]{2,1,0:T(8,128)(2,1)} %collective-permute-done.f_l), channel_id=1, source_target_pairs={{0,1},{1,0},{2,3},{3,2},{4,5},{5,4},{6,7},{7,6},{8,9},{9,8},{10,11... | collective-permute-start | bytes 3145736 | tf_op jit(solution)/shard_map/ppermute | solution.py:21
  80.5 31.0 %collective-permute-start.9 = (bf16[2,256,256]{2,1,0:T(8,128)(2,1)}, bf16[2,256,256]{2,1,0:T(8,128)(2,1)S(1)}, u32[]{:S(2)}, u32[]{:S(2)}) collective-permute-start(bf16[2,256,256]{2,1,0:T(8,128)(2,1)} %slice.24), channel_id=1, source_target_pairs={{2,0},{6,4},{10,8},{14,12},{18,16},{22,20},{26,24},{30,28},{3,1},{... | collective-permute-start | bytes 786440 | tf_op jit(solution)/shard_map/ppermute | solution.py:17
  91.0 21.3 %collective-permute-start.8 = (bf16[2,128,256]{2,1,0:T(8,128)(2,1)S(1)}, bf16[2,128,256]{2,1,0:T(8,128)(2,1)S(1)}, u32[]{:S(2)}, u32[]{:S(2)}) collective-permute-start(bf16[2,128,256]{2,1,0:T(8,128)(2,1)S(1)} %get-tuple-element.8), channel_id=1, source_target_pairs={{2,0},{6,4},{10,8},{14,12},{18,16},{22,20},{26,24},{30,28},{3,1},{... | collective-permute-start | bytes 393224 | tf_op jit(solution)/shard_map/ppermute | solution.py:17
  92.3 23.8 %collective-permute-start.7 = (bf16[2,128,256]{2,1,0:T(8,128)(2,1)S(1)}, bf16[2,128,256]{2,1,0:T(8,128)(2,1)S(1)}, u32[]{:S(2)}, u32[]{:S(2)}) collective-permute-start(bf16[2,128,256]{2,1,0:T(8,128)(2,1)S(1)} %get-tuple-element.9), channel_id=1, source_target_pairs={{2,0},{6,4},{10,8},{14,12},{18,16},{22,20},{26,24},{30,28},{3,1},{... | collective-permute-start | bytes 393224 | tf_op jit(solution)/shard_map/ppermute | solution.py:17
  93.8 1.2 %copy-start.7 = (bf16[1,1,2,512,512]{4,3,2,1,0:T(8,128)(2,1)S(1)}, bf16[1,1,2,512,512]{4,3,2,1,0:T(8,128)(2,1)}, u32[]{:S(2)}) copy-start(bf16[1,1,2,512,512]{4,3,2,1,0:T(8,128)(2,1)} %param.7) | copy-start | bytes 3145732
  95.0 1.2 %copy-start.10 = (bf16[2,512,512]{2,1,0:T(8,128)(2,1)S(1)}, bf16[2,512,512]{2,1,0:T(8,128)(2,1)}, u32[]{:S(2)}) copy-start(bf16[2,512,512]{2,1,0:T(8,128)(2,1)} %copy-done.8) | copy-start | bytes 3145732
  96.2 1.2 %copy-start.12 = (bf16[2,512,512]{2,1,0:T(8,128)(2,1)S(1)}, bf16[2,512,512]{2,1,0:T(8,128)(2,1)}, u32[]{:S(2)}) copy-start(bf16[2,512,512]{2,1,0:T(8,128)(2,1)} %copy-done.11) | copy-start | bytes 3145732
  97.4 1.2 %copy-start.14 = (bf16[2,512,512]{2,1,0:T(8,128)(2,1)S(1)}, bf16[2,512,512]{2,1,0:T(8,128)(2,1)}, u32[]{:S(2)}) copy-start(bf16[2,512,512]{2,1,0:T(8,128)(2,1)} %copy-done.13) | copy-start | bytes 3145732
  98.7 1.2 %copy-start.16 = (bf16[2,512,512]{2,1,0:T(8,128)(2,1)S(1)}, bf16[2,512,512]{2,1,0:T(8,128)(2,1)}, u32[]{:S(2)}) copy-start(bf16[2,512,512]{2,1,0:T(8,128)(2,1)} %copy-done.15) | copy-start | bytes 3145732
  99.9 1.2 %copy-start.18 = (bf16[2,512,512]{2,1,0:T(8,128)(2,1)S(1)}, bf16[2,512,512]{2,1,0:T(8,128)(2,1)}, u32[]{:S(2)}) copy-start(bf16[2,512,512]{2,1,0:T(8,128)(2,1)} %copy-done.17) | copy-start | bytes 3145732
  101.1 1.2 %copy-start.20 = (bf16[2,512,512]{2,1,0:T(8,128)(2,1)S(1)}, bf16[2,512,512]{2,1,0:T(8,128)(2,1)}, u32[]{:S(2)}) copy-start(bf16[2,512,512]{2,1,0:T(8,128)(2,1)} %copy-done.19) | copy-start | bytes 3145732
